TPU v7x, 32 devices: a whole 2x2x4 slice. The times are simulated.
32 devices in a mesh: section: 2 (over y), expert: 8 (over z, x), dp: 2 (over core).
Axes of the slice: x: 2, y: 2, z: 4, core: 2. Of those that a mesh axis runs over, the one named last changes fastest.
Arguments:
- tokens_in: bfloat16 [8, 256, 2048], P(None, ('expert', 'dp')), may hold values from -6 to 6
- cotangent: bfloat16 [8, 256, 2048], P(None, ('expert', 'dp')), may hold values from -4 to 4
- routes: int32 [2, 8, 256, 8], P('section', None, ('expert', 'dp')), may hold values from 0 to 15, all different within a row; in each aligned block of 16 rows (0 to 15, 16 to 31, ..., all dimensions but the last counted through in order) at most 10 rows name the same one
- router_weights: float32 [2, 8, 256, 8], P('section', None, ('expert', 'dp')), may hold values from 0.1 to 0.6
- norm_gain: float32 [2, 2048], P('section'), may hold values from 0.25 to 1.75
- w_gate: bfloat16 [2, 16, 2048, 512], P('section', 'expert'), may hold values from -0.125 to 0.125
- w_up: bfloat16 [2, 16, 2048, 512], P('section', 'expert'), may hold values from -0.125 to 0.125
- w_down: bfloat16 [2, 16, 512, 2048], P('section', 'expert'), may hold values from -0.25 to 0.25
Outputs:
- layer_out: bfloat16 [2, 8, 256, 2048], P('section', None, ('expert', 'dp'))
- input_grad: bfloat16 [2, 8, 256, 2048], P('section', None, ('expert', 'dp'))
- grad_gate: bfloat16 [2, 16, 2048, 512], P('section', 'expert', 'dp')
- grad_up: bfloat16 [2, 16, 2048, 512], P('section', 'expert', 'dp')
- grad_down: bfloat16 [2, 16, 512, 2048], P('section', 'expert', 'dp')
Inputs may be any that keep to these rules, and one draw needn't show every extreme that they name: `routes`: each row names 8 different experts. In each aligned block of 16 rows (the tokens of one device for one layer and one micro-batch) no expert is named by more than 10 rows, and in some blocks one is named by exactly 10.
All inputs are finite; a program needn't handle non-finite values.
Results may differ from a plain program's by a relative error of at most 0.022.
Values may be sent and summed in bfloat16 or wider, within the bound.
A program may use at most 128 MiB of HBM per device.

v0:
```python
import jax
import jax.numpy as jnp
from jax import lax
from jax.sharding import PartitionSpec as P

epsilon = 1e-06


def from_behind(block, axis, distance):
    devices = range(lax.axis_size(axis))
    route = [(i - distance, i) for i in devices if i - distance in devices]
    return lax.ppermute(block, axis, route)


def normalize(hidden, gain_row):
    widened = hidden.astype(jnp.float32)
    inv_rms = lax.rsqrt(jnp.mean(widened * widened, axis=-1, keepdims=True) + epsilon)
    return ((widened * inv_rms * gain_row).astype(jnp.bfloat16), widened, inv_rms)


def routing_tables(route_ids, route_weights, capacity, experts):
    micro_count, token_rows, top_count = route_ids.shape
    assigned = token_rows * top_count
    flat_ids = route_ids.reshape(micro_count, assigned)
    labels = jnp.arange(experts, dtype=jnp.int32)
    onehot = (flat_ids[:, :, None] == labels[None, None, :]).astype(jnp.int32)
    earlier = jnp.cumsum(onehot, axis=1) - onehot
    position = jnp.sum(earlier * onehot, axis=2)
    target = flat_ids * capacity + position
    places = jnp.arange(experts * capacity, dtype=jnp.int32)
    matched = (target[:, None, :] == places[None, :, None]).reshape(
        micro_count, experts * capacity, token_rows, top_count
    )
    selector = jnp.any(matched, axis=3).astype(jnp.bfloat16)
    weighted = jnp.sum(jnp.where(matched, route_weights[:, None, :, :], 0.0), axis=3)
    return (selector, weighted)


def expert_forward(rows_in, gate_w, up_w, down_w):
    gate_pre = jnp.einsum("erx,exf->erf", rows_in, gate_w, preferred_element_type=jnp.float32)
    up_pre = jnp.einsum("erx,exf->erf", rows_in, up_w, preferred_element_type=jnp.float32)
    act_value = (jax.nn.silu(gate_pre) * up_pre).astype(jnp.bfloat16)
    produced = jnp.einsum(
        "erf,efx->erx", act_value, down_w, preferred_element_type=jnp.float32
    ).astype(jnp.bfloat16)
    return (produced, gate_pre, up_pre)


def expert_backward(out_grad, gate_pre, up_pre, gate_w, up_w, down_w):
    act_grad = jnp.einsum("erx,efx->erf", out_grad, down_w, preferred_element_type=jnp.float32)
    sigmoid_g = jax.nn.sigmoid(gate_pre)
    up_grad = (act_grad * gate_pre * sigmoid_g).astype(jnp.bfloat16)
    gate_grad = (act_grad * up_pre * sigmoid_g * (1.0 + gate_pre * (1.0 - sigmoid_g))).astype(
        jnp.bfloat16
    )
    row_grad = jnp.einsum("erf,exf->erx", gate_grad, gate_w, preferred_element_type=jnp.float32)
    row_grad = row_grad + jnp.einsum(
        "erf,exf->erx", up_grad, up_w, preferred_element_type=jnp.float32
    )
    return (row_grad.astype(jnp.bfloat16), gate_grad, up_grad)


def keep_slice(stored, new_value, at_index, is_valid):
    previous = lax.dynamic_index_in_dim(stored, at_index, 0, keepdims=False)
    return lax.dynamic_update_index_in_dim(
        stored, jnp.where(is_valid, new_value, previous), at_index, 0
    )


def round_part(partial_value):
    return lax.optimization_barrier(partial_value.astype(jnp.bfloat16)).astype(jnp.float32)


def send_out(buffer):
    return lax.all_to_all(buffer, "expert", split_axis=0, concat_axis=1, tiled=True)


def send_back(buffer):
    return lax.all_to_all(buffer, "expert", split_axis=1, concat_axis=0, tiled=True)


def on_device(tokens_in, cotangent, routes, router_weights, norm_gain, w_gate, w_up, w_down):
    micro_count, token_rows, model_width = tokens_in.shape
    top_count = routes.shape[3]
    hidden_units = w_gate.shape[3]
    section_count = lax.axis_size("section")
    expert_count = lax.axis_size("expert")
    held_count = w_gate.shape[1]
    experts = held_count * expert_count
    capacity = min(token_rows, 5 * token_rows * top_count // (4 * experts))
    slot_count = experts * capacity
    section_id = lax.axis_index("section")
    selector, weighted = routing_tables(routes[0], router_weights[0], capacity, experts)
    slot_weight = jnp.sum(weighted, axis=2)
    gain_row = norm_gain[0]
    gate_local = w_gate[0]
    up_local = w_up[0]
    down_local = w_down[0]
    expert_rows = expert_count * capacity
    tick_count = section_count + micro_count - 1

    def forward_tick(tick_id, loop_state):
        incoming, inputs_kept, rows_kept, gate_kept, up_kept, outputs_kept = loop_state
        micro_id = tick_id - section_id
        is_valid = jnp.logical_and(micro_id >= 0, micro_id < micro_count)
        clipped = jnp.clip(micro_id, 0, micro_count - 1)
        fresh_in = lax.dynamic_index_in_dim(tokens_in, clipped, 0, keepdims=False)
        hidden = jnp.where(section_id == 0, fresh_in, incoming)
        normed, widened, inv_rms = normalize(hidden, gain_row)
        chooser = lax.dynamic_index_in_dim(selector, clipped, 0, keepdims=False)
        spread = jnp.dot(chooser, normed, preferred_element_type=jnp.float32).astype(jnp.bfloat16)
        arrived = send_out(spread.reshape(experts, capacity, model_width))

        def forward_compute(rows_in):
            return expert_forward(rows_in, gate_local, up_local, down_local)

        def forward_skipped(rows_in):
            return (
                jnp.zeros((held_count, expert_rows, model_width), jnp.bfloat16),
                jnp.zeros((held_count, expert_rows, hidden_units), jnp.float32),
                jnp.zeros((held_count, expert_rows, hidden_units), jnp.float32),
            )

        produced, gate_value, up_value = lax.cond(
            is_valid, forward_compute, forward_skipped, arrived
        )
        returned = send_back(produced).reshape(slot_count, model_width)
        mix_table = lax.dynamic_index_in_dim(weighted, clipped, 0, keepdims=False)
        mixed_sum = widened + jnp.dot(
            mix_table.T,
            returned.astype(jnp.float32),
            precision=lax.Precision.HIGHEST,
            preferred_element_type=jnp.float32,
        )
        output = mixed_sum.astype(jnp.bfloat16)
        inputs_kept = keep_slice(inputs_kept, hidden, clipped, is_valid)
        rows_kept = keep_slice(rows_kept, arrived, clipped, is_valid)
        gate_kept = keep_slice(gate_kept, gate_value, clipped, is_valid)
        up_kept = keep_slice(up_kept, up_value, clipped, is_valid)
        outputs_kept = keep_slice(outputs_kept, output, clipped, is_valid)
        outgoing = from_behind(output, "section", 1)
        return (outgoing, inputs_kept, rows_kept, gate_kept, up_kept, outputs_kept)

    start_state = (
        jnp.zeros((token_rows, model_width), jnp.bfloat16),
        jnp.zeros((micro_count, token_rows, model_width), jnp.bfloat16),
        jnp.zeros((micro_count, held_count, expert_rows, model_width), jnp.bfloat16),
        jnp.zeros((micro_count, held_count, expert_rows, hidden_units), jnp.float32),
        jnp.zeros((micro_count, held_count, expert_rows, hidden_units), jnp.float32),
        jnp.zeros((micro_count, token_rows, model_width), jnp.bfloat16),
    )
    forward_state = lax.fori_loop(0, tick_count, forward_tick, start_state)
    inputs_kept = forward_state[1]
    rows_kept = forward_state[2]
    gate_kept = forward_state[3]
    up_kept = forward_state[4]
    outputs_kept = forward_state[5]

    def backward_tick(tick_id, loop_state):
        incoming, out_kept, gate_grads_kept, up_grads_kept, grads_kept = loop_state
        micro_id = tick_id - (section_count - 1 - section_id)
        is_valid = jnp.logical_and(micro_id >= 0, micro_id < micro_count)
        clipped = jnp.clip(micro_id, 0, micro_count - 1)
        fresh_in = lax.dynamic_index_in_dim(cotangent, clipped, 0, keepdims=False)
        grad_out = jnp.where(section_id == section_count - 1, fresh_in, incoming)
        chooser = lax.dynamic_index_in_dim(selector, clipped, 0, keepdims=False)
        gathered = jnp.dot(chooser, grad_out, preferred_element_type=jnp.float32)
        weight_col = lax.dynamic_index_in_dim(slot_weight, clipped, 0, keepdims=False)
        out_grad = (weight_col[:, None] * gathered).astype(jnp.bfloat16)
        arrived = send_out(out_grad.reshape(experts, capacity, model_width))
        gate_value = lax.dynamic_index_in_dim(gate_kept, clipped, 0, keepdims=False)
        up_value = lax.dynamic_index_in_dim(up_kept, clipped, 0, keepdims=False)

        def backward_compute(operands):
            return expert_backward(
                operands[0], operands[1], operands[2], gate_local, up_local, down_local
            )

        def backward_skipped(operands):
            return (
                jnp.zeros((held_count, expert_rows, model_width), jnp.bfloat16),
                jnp.zeros((held_count, expert_rows, hidden_units), jnp.bfloat16),
                jnp.zeros((held_count, expert_rows, hidden_units), jnp.bfloat16),
            )

        row_grad, gate_grad, up_grad = lax.cond(
            is_valid, backward_compute, backward_skipped, (arrived, gate_value, up_value)
        )
        backed = send_back(row_grad).reshape(slot_count, model_width)
        dnormed = jnp.dot(chooser.T, backed, preferred_element_type=jnp.float32)
        hidden = lax.dynamic_index_in_dim(inputs_kept, clipped, 0, keepdims=False)
        widened = hidden.astype(jnp.float32)
        inv_rms = lax.rsqrt(jnp.mean(widened * widened, axis=-1, keepdims=True) + epsilon)
        unit_rows = widened * inv_rms
        scaled = dnormed * gain_row
        dhidden = grad_out.astype(jnp.float32) + inv_rms * (
            scaled - unit_rows * jnp.mean(scaled * unit_rows, axis=-1, keepdims=True)
        )
        result = dhidden.astype(jnp.bfloat16)
        out_kept = keep_slice(out_kept, arrived, clipped, is_valid)
        gate_grads_kept = keep_slice(gate_grads_kept, gate_grad, clipped, is_valid)
        up_grads_kept = keep_slice(up_grads_kept, up_grad, clipped, is_valid)
        grads_kept = keep_slice(grads_kept, result, clipped, is_valid)
        outgoing = from_behind(result, "section", -1)
        return (outgoing, out_kept, gate_grads_kept, up_grads_kept, grads_kept)

    back_start = (
        jnp.zeros((token_rows, model_width), jnp.bfloat16),
        jnp.zeros((micro_count, held_count, expert_rows, model_width), jnp.bfloat16),
        jnp.zeros((micro_count, held_count, expert_rows, hidden_units), jnp.bfloat16),
        jnp.zeros((micro_count, held_count, expert_rows, hidden_units), jnp.bfloat16),
        jnp.zeros((micro_count, token_rows, model_width), jnp.bfloat16),
    )
    back_state = lax.fori_loop(0, tick_count, backward_tick, back_start)
    out_kept = back_state[1]
    gate_grads_kept = back_state[2]
    up_grads_kept = back_state[3]
    grads_kept = back_state[4]
    act_all = (jax.nn.silu(gate_kept) * up_kept).astype(jnp.bfloat16)
    part_gate = jnp.einsum(
        "merx,merf->exf", rows_kept, gate_grads_kept, preferred_element_type=jnp.float32
    )
    part_up = jnp.einsum(
        "merx,merf->exf", rows_kept, up_grads_kept, preferred_element_type=jnp.float32
    )
    part_down = jnp.einsum("merf,merx->efx", act_all, out_kept, preferred_element_type=jnp.float32)
    summed = (
        lax.psum_scatter(
            round_part(part_gate).astype(jnp.bfloat16), "dp", scatter_dimension=1, tiled=True
        ).astype(jnp.float32),
        lax.psum_scatter(
            round_part(part_up).astype(jnp.bfloat16), "dp", scatter_dimension=1, tiled=True
        ).astype(jnp.float32),
        lax.psum_scatter(
            round_part(part_down).astype(jnp.bfloat16), "dp", scatter_dimension=1, tiled=True
        ).astype(jnp.float32),
    )
    grad_gate = summed[0].astype(jnp.bfloat16)
    grad_up = summed[1].astype(jnp.bfloat16)
    grad_down = summed[2].astype(jnp.bfloat16)
    return (outputs_kept[None], grads_kept[None], grad_gate[None], grad_up[None], grad_down[None])


def solution(mesh):
    placed = (
        P(None, ("expert", "dp"), None),
        P(None, ("expert", "dp"), None),
        P("section", None, ("expert", "dp"), None),
        P("section", None, ("expert", "dp"), None),
        P("section", None),
        P("section", "expert", None, None),
        P("section", "expert", None, None),
        P("section", "expert", None, None),
    )
    return jax.shard_map(
        on_device,
        mesh=mesh,
        in_specs=placed,
        out_specs=(
            P("section", None, ("expert", "dp"), None),
            P("section", None, ("expert", "dp"), None),
            P("section", "expert", "dp", None),
            P("section", "expert", "dp", None),
            P("section", "expert", "dp", None),
        ),
        check_vma=False,
    )
```

profile of v0, /device:TPU:0, one launch (start us, length us, event | category | flops | bytes accessed | tf_op | source)
XLA Modules:
  0.0 1394.0 jit_solution(1228539044011185446)
XLA Ops:
  21.6 651.4 %while.47 = (s32[]{:T(128)}, bf16[16,2048]{1,0:T(8,128)(2,1)S(1)}, bf16[8,16,2048]{2,1,0:T(8,128)(2,1)}, bf16[8,2,80,2048]{3,2,0,1:T(8,128)(2,1)}, f32[8,2,80,51...) while((s32[]{:T(128)}, bf16[16,2048]{1,0:T(8,128)(2,1)S(1)}, ...), condition=%wide.region_8.9_spmd, body=%wide.region_4.0_spmd.sunk | while | flops 1082097664 | bytes 73764016 | solution.py:152
  25.7 7.3 all-to-all-start
  34.9 23.8 %all-to-all-done = bf16[16,10,2048]{2,1,0:T(8,128)(2,1)S(1)} async-done(((bf16[16,10,2048]{2,1,0:T(8,128)(2,1)}), bf16[16,10,2048]{2,1,0:T(8,128)(2,1)S(1)}, u32[]{:S(2)}, u32[]{:S(2)}) %all-to-all-start) | async-done | bytes 655392 | tf_op jit(solution)/shard_map/while/body/eval_jaxpr/all_to_all | solution.py:75
  59.4 8.7 conditional.4
  77.8 12.8 all-to-all-done.1
  105.2 24.0 %all-to-all-done = bf16[16,10,2048]{2,1,0:T(8,128)(2,1)S(1)} async-done(((bf16[16,10,2048]{2,1,0:T(8,128)(2,1)}), bf16[16,10,2048]{2,1,0:T(8,128)(2,1)S(1)}, u32[]{:S(2)}, u32[]{:S(2)}) %all-to-all-start) | async-done | bytes 655392 | tf_op jit(solution)/shard_map/while/body/eval_jaxpr/all_to_all | solution.py:75
  129.9 8.7 conditional.4
  148.3 12.9 all-to-all-done.1
  177.9 23.7 %all-to-all-done = bf16[16,10,2048]{2,1,0:T(8,128)(2,1)S(1)} async-done(((bf16[16,10,2048]{2,1,0:T(8,128)(2,1)}), bf16[16,10,2048]{2,1,0:T(8,128)(2,1)S(1)}, u32[]{:S(2)}, u32[]{:S(2)}) %all-to-all-start) | async-done | bytes 655392 | tf_op jit(solution)/shard_map/while/body/eval_jaxpr/all_to_all | solution.py:75
  202.3 8.7 conditional.4
  220.7 12.9 all-to-all-done.1
  250.1 23.7 %all-to-all-done = bf16[16,10,2048]{2,1,0:T(8,128)(2,1)S(1)} async-done(((bf16[16,10,2048]{2,1,0:T(8,128)(2,1)}), bf16[16,10,2048]{2,1,0:T(8,128)(2,1)S(1)}, u32[]{:S(2)}, u32[]{:S(2)}) %all-to-all-start) | async-done | bytes 655392 | tf_op jit(solution)/shard_map/while/body/eval_jaxpr/all_to_all | solution.py:75
  274.5 8.7 conditional.4
  292.9 12.9 all-to-all-done.1
  322.2 23.7 %all-to-all-done = bf16[16,10,2048]{2,1,0:T(8,128)(2,1)S(1)} async-done(((bf16[16,10,2048]{2,1,0:T(8,128)(2,1)}), bf16[16,10,2048]{2,1,0:T(8,128)(2,1)S(1)}, u32[]{:S(2)}, u32[]{:S(2)}) %all-to-all-start) | async-done | bytes 655392 | tf_op jit(solution)/shard_map/while/body/eval_jaxpr/all_to_all | solution.py:75
  346.6 8.7 conditional.4
  365.0 12.9 all-to-all-done.1
  394.3 23.7 %all-to-all-done = bf16[16,10,2048]{2,1,0:T(8,128)(2,1)S(1)} async-done(((bf16[16,10,2048]{2,1,0:T(8,128)(2,1)}), bf16[16,10,2048]{2,1,0:T(8,128)(2,1)S(1)}, u32[]{:S(2)}, u32[]{:S(2)}) %all-to-all-start) | async-done | bytes 655392 | tf_op jit(solution)/shard_map/while/body/eval_jaxpr/all_to_all | solution.py:75
  418.7 8.7 conditional.4
  437.1 12.8 all-to-all-done.1
  466.5 23.7 %all-to-all-done = bf16[16,10,2048]{2,1,0:T(8,128)(2,1)S(1)} async-done(((bf16[16,10,2048]{2,1,0:T(8,128)(2,1)}), bf16[16,10,2048]{2,1,0:T(8,128)(2,1)S(1)}, u32[]{:S(2)}, u32[]{:S(2)}) %all-to-all-start) | async-done | bytes 655392 | tf_op jit(solution)/shard_map/while/body/eval_jaxpr/all_to_all | solution.py:75
  490.9 8.7 conditional.4
  509.3 12.9 all-to-all-done.1
  538.6 23.7 %all-to-all-done = bf16[16,10,2048]{2,1,0:T(8,128)(2,1)S(1)} async-done(((bf16[16,10,2048]{2,1,0:T(8,128)(2,1)}), bf16[16,10,2048]{2,1,0:T(8,128)(2,1)S(1)}, u32[]{:S(2)}, u32[]{:S(2)}) %all-to-all-start) | async-done | bytes 655392 | tf_op jit(solution)/shard_map/while/body/eval_jaxpr/all_to_all | solution.py:75
  563.0 8.7 conditional.4
  581.4 12.9 all-to-all-done.1
  610.8 23.7 %all-to-all-done = bf16[16,10,2048]{2,1,0:T(8,128)(2,1)S(1)} async-done(((bf16[16,10,2048]{2,1,0:T(8,128)(2,1)}), bf16[16,10,2048]{2,1,0:T(8,128)(2,1)S(1)}, u32[]{:S(2)}, u32[]{:S(2)}) %all-to-all-start) | async-done | bytes 655392 | tf_op jit(solution)/shard_map/while/body/eval_jaxpr/all_to_all | solution.py:75
  646.5 12.9 all-to-all-done.1
  660.9 10.3 collective-permute-start
  678.5 657.6 %while.48 = (s32[]{:T(128)}, bf16[16,2048]{1,0:T(8,128)(2,1)S(1)}, bf16[8,2,80,2048]{3,2,1,0:T(8,128)(2,1)}, bf16[8,2,80,512]{3,2,0,1:T(8,128)(2,1)}, bf16[8,2,8...) while((s32[]{:T(128)}, bf16[16,2048]{1,0:T(8,128)(2,1)S(1)}, ...), condition=%wide.region_15.16_spmd, body=%wide.region_10.15_spmd.sunk | while | flops 1031094272 | bytes 74154120 | solution.py:214
  686.7 23.2 %all-to-all-done.2 = bf16[16,10,2048]{2,1,0:T(8,128)(2,1)S(1)} async-done(((bf16[16,10,2048]{2,1,0:T(8,128)(2,1)}), bf16[16,10,2048]{2,1,0:T(8,128)(2,1)S(1)}, u32[]{:S(2)}, u32[]{:S(2)}) %all-to-all-start.2) | async-done | bytes 655392 | tf_op jit(solution)/shard_map/while/body/eval_jaxpr/all_to_all | solution.py:75
  721.5 12.8 all-to-all-done.3
  739.1 12.1 collective-permute-done.1
  759.4 23.4 %all-to-all-done.2 = bf16[16,10,2048]{2,1,0:T(8,128)(2,1)S(1)} async-done(((bf16[16,10,2048]{2,1,0:T(8,128)(2,1)}), bf16[16,10,2048]{2,1,0:T(8,128)(2,1)S(1)}, u32[]{:S(2)}, u32[]{:S(2)}) %all-to-all-start.2) | async-done | bytes 655392 | tf_op jit(solution)/shard_map/while/body/eval_jaxpr/all_to_all | solution.py:75
  783.5 10.1 conditional.5
  803.2 12.8 all-to-all-done.3
  833.0 22.9 %all-to-all-done.2 = bf16[16,10,2048]{2,1,0:T(8,128)(2,1)S(1)} async-done(((bf16[16,10,2048]{2,1,0:T(8,128)(2,1)}), bf16[16,10,2048]{2,1,0:T(8,128)(2,1)S(1)}, u32[]{:S(2)}, u32[]{:S(2)}) %all-to-all-start.2) | async-done | bytes 655392 | tf_op jit(solution)/shard_map/while/body/eval_jaxpr/all_to_all | solution.py:75
  856.6 10.1 conditional.5
  857.1 4.8 fusion.29
  876.3 12.8 all-to-all-done.3
  906.1 22.9 %all-to-all-done.2 = bf16[16,10,2048]{2,1,0:T(8,128)(2,1)S(1)} async-done(((bf16[16,10,2048]{2,1,0:T(8,128)(2,1)}), bf16[16,10,2048]{2,1,0:T(8,128)(2,1)S(1)}, u32[]{:S(2)}, u32[]{:S(2)}) %all-to-all-start.2) | async-done | bytes 655392 | tf_op jit(solution)/shard_map/while/body/eval_jaxpr/all_to_all | solution.py:75
  929.6 10.1 conditional.5
  949.3 12.8 all-to-all-done.3
  979.1 22.9 %all-to-all-done.2 = bf16[16,10,2048]{2,1,0:T(8,128)(2,1)S(1)} async-done(((bf16[16,10,2048]{2,1,0:T(8,128)(2,1)}), bf16[16,10,2048]{2,1,0:T(8,128)(2,1)S(1)}, u32[]{:S(2)}, u32[]{:S(2)}) %all-to-all-start.2) | async-done | bytes 655392 | tf_op jit(solution)/shard_map/while/body/eval_jaxpr/all_to_all | solution.py:75
  1002.7 10.1 conditional.5
  1003.2 4.8 fusion.29
  1022.3 12.9 all-to-all-done.3
  1052.1 22.9 %all-to-all-done.2 = bf16[16,10,2048]{2,1,0:T(8,128)(2,1)S(1)} async-done(((bf16[16,10,2048]{2,1,0:T(8,128)(2,1)}), bf16[16,10,2048]{2,1,0:T(8,128)(2,1)S(1)}, u32[]{:S(2)}, u32[]{:S(2)}) %all-to-all-start.2) | async-done | bytes 655392 | tf_op jit(solution)/shard_map/while/body/eval_jaxpr/all_to_all | solution.py:75
  1075.7 10.1 conditional.5
  1095.4 12.8 all-to-all-done.3
  1125.2 22.9 %all-to-all-done.2 = bf16[16,10,2048]{2,1,0:T(8,128)(2,1)S(1)} async-done(((bf16[16,10,2048]{2,1,0:T(8,128)(2,1)}), bf16[16,10,2048]{2,1,0:T(8,128)(2,1)S(1)}, u32[]{:S(2)}, u32[]{:S(2)}) %all-to-all-start.2) | async-done | bytes 655392 | tf_op jit(solution)/shard_map/while/body/eval_jaxpr/all_to_all | solution.py:75
  1148.7 10.1 conditional.5
  1168.5 12.8 all-to-all-done.3
  1198.2 22.9 %all-to-all-done.2 = bf16[16,10,2048]{2,1,0:T(8,128)(2,1)S(1)} async-done(((bf16[16,10,2048]{2,1,0:T(8,128)(2,1)}), bf16[16,10,2048]{2,1,0:T(8,128)(2,1)S(1)}, u32[]{:S(2)}, u32[]{:S(2)}) %all-to-all-start.2) | async-done | bytes 655392 | tf_op jit(solution)/shard_map/while/body/eval_jaxpr/all_to_all | solution.py:75
  1221.8 10.1 conditional.5
  1241.4 12.8 all-to-all-done.3
  1271.3 22.9 %all-to-all-done.2 = bf16[16,10,2048]{2,1,0:T(8,128)(2,1)S(1)} async-done(((bf16[16,10,2048]{2,1,0:T(8,128)(2,1)}), bf16[16,10,2048]{2,1,0:T(8,128)(2,1)S(1)}, u32[]{:S(2)}, u32[]{:S(2)}) %all-to-all-start.2) | async-done | bytes 655392 | tf_op jit(solution)/shard_map/while/body/eval_jaxpr/all_to_all | solution.py:75
  1294.8 10.1 conditional.5
  1314.4 12.9 all-to-all-done.3
  1336.1 8.5 bitcast_convert_fusion.1
  1346.0 8.4 bitcast_convert_fusion.2
  1356.2 8.8 bitcast_convert_fusion
  1365.0 6.2 reduce-scatter.4.cloned.1.call-done
  1371.2 16.2 %reduce-scatter.8.cloned.1.call-done = bf16[2,256,2048]{2,1,0:T(8,128)(2,1)} async-done(((bf16[2,512,2048]{2,1,0:T(8,128)(2,1)}), bf16[2,256,2048]{2,1,0:T(8,128)(2,1)}) %reduce-scatter.8.cloned.1.call-update) | async-done | bytes 2097168 | tf_op jit(solution)/shard_map/reduce_scatter | solution.py:234
  (589 shorter events, 641.9 us)
Async XLA Ops:
  7.2 1357.9 %reduce-scatter.6.cloned.1.call-start = ((), (), s32[]{:S(2)}) async-start(), calls=%async_computation.8 | async-start | bytes 6291456 | tf_op jit(solution)/shard_map/reduce_scatter | solution.py:231
  25.7 33.0 %all-to-all-start = ((bf16[16,10,2048]{2,1,0:T(8,128)(2,1)}), bf16[16,10,2048]{2,1,0:T(8,128)(2,1)S(1)}, u32[]{:S(2)}, u32[]{:S(2)}) async-start(bf16[16,10,2048]{2,1,0:T(8,128)(2,1)} %reshape.112), calls=%async_computation | async-start | bytes 2097152 | tf_op jit(solution)/shard_map/while/body/eval_jaxpr/all_to_all | solution.py:75
  69.6 21.1 %all-to-all-start.1 = ((bf16[2,80,2048]{2,0,1:T(2,128)(2,1)}), bf16[2,80,2048]{2,0,1:T(2,128)(2,1)S(1)}, u32[]{:S(2)}, u32[]{:S(2)}) async-start(bf16[2,80,2048]{2,0,1:T(2,128)(2,1)} %copy.142), calls=%async_computation.1 | async-start | bytes 1310720 | tf_op jit(solution)/shard_map/while/body/eval_jaxpr/all_to_all | solution.py:79
  92.2 3.3 collective-permute-start
  99.6 29.6 %all-to-all-start = ((bf16[16,10,2048]{2,1,0:T(8,128)(2,1)}), bf16[16,10,2048]{2,1,0:T(8,128)(2,1)S(1)}, u32[]{:S(2)}, u32[]{:S(2)}) async-start(bf16[16,10,2048]{2,1,0:T(8,128)(2,1)} %reshape.112), calls=%async_computation | async-start | bytes 2097152 | tf_op jit(solution)/shard_map/while/body/eval_jaxpr/all_to_all | solution.py:75
  140.1 21.1 %all-to-all-start.1 = ((bf16[2,80,2048]{2,0,1:T(2,128)(2,1)}), bf16[2,80,2048]{2,0,1:T(2,128)(2,1)S(1)}, u32[]{:S(2)}, u32[]{:S(2)}) async-start(bf16[2,80,2048]{2,0,1:T(2,128)(2,1)} %copy.142), calls=%async_computation.1 | async-start | bytes 1310720 | tf_op jit(solution)/shard_map/while/body/eval_jaxpr/all_to_all | solution.py:79
  162.7 5.5 collective-permute-start
  172.3 29.3 %all-to-all-start = ((bf16[16,10,2048]{2,1,0:T(8,128)(2,1)}), bf16[16,10,2048]{2,1,0:T(8,128)(2,1)S(1)}, u32[]{:S(2)}, u32[]{:S(2)}) async-start(bf16[16,10,2048]{2,1,0:T(8,128)(2,1)} %reshape.112), calls=%async_computation | async-start | bytes 2097152 | tf_op jit(solution)/shard_map/while/body/eval_jaxpr/all_to_all | solution.py:75
  212.5 21.0 %all-to-all-start.1 = ((bf16[2,80,2048]{2,0,1:T(2,128)(2,1)}), bf16[2,80,2048]{2,0,1:T(2,128)(2,1)S(1)}, u32[]{:S(2)}, u32[]{:S(2)}) async-start(bf16[2,80,2048]{2,0,1:T(2,128)(2,1)} %copy.142), calls=%async_computation.1 | async-start | bytes 1310720 | tf_op jit(solution)/shard_map/while/body/eval_jaxpr/all_to_all | solution.py:79
  235.1 5.4 collective-permute-start
  244.5 29.3 %all-to-all-start = ((bf16[16,10,2048]{2,1,0:T(8,128)(2,1)}), bf16[16,10,2048]{2,1,0:T(8,128)(2,1)S(1)}, u32[]{:S(2)}, u32[]{:S(2)}) async-start(bf16[16,10,2048]{2,1,0:T(8,128)(2,1)} %reshape.112), calls=%async_computation | async-start | bytes 2097152 | tf_op jit(solution)/shard_map/while/body/eval_jaxpr/all_to_all | solution.py:75
  284.8 21.0 %all-to-all-start.1 = ((bf16[2,80,2048]{2,0,1:T(2,128)(2,1)}), bf16[2,80,2048]{2,0,1:T(2,128)(2,1)S(1)}, u32[]{:S(2)}, u32[]{:S(2)}) async-start(bf16[2,80,2048]{2,0,1:T(2,128)(2,1)} %copy.142), calls=%async_computation.1 | async-start | bytes 1310720 | tf_op jit(solution)/shard_map/while/body/eval_jaxpr/all_to_all | solution.py:79
  307.3 5.2 collective-permute-start
  316.6 29.3 %all-to-all-start = ((bf16[16,10,2048]{2,1,0:T(8,128)(2,1)}), bf16[16,10,2048]{2,1,0:T(8,128)(2,1)S(1)}, u32[]{:S(2)}, u32[]{:S(2)}) async-start(bf16[16,10,2048]{2,1,0:T(8,128)(2,1)} %reshape.112), calls=%async_computation | async-start | bytes 2097152 | tf_op jit(solution)/shard_map/while/body/eval_jaxpr/all_to_all | solution.py:75
  356.8 21.0 %all-to-all-start.1 = ((bf16[2,80,2048]{2,0,1:T(2,128)(2,1)}), bf16[2,80,2048]{2,0,1:T(2,128)(2,1)S(1)}, u32[]{:S(2)}, u32[]{:S(2)}) async-start(bf16[2,80,2048]{2,0,1:T(2,128)(2,1)} %copy.142), calls=%async_computation.1 | async-start | bytes 1310720 | tf_op jit(solution)/shard_map/while/body/eval_jaxpr/all_to_all | solution.py:79
  379.4 5.3 collective-permute-start
  388.7 29.3 %all-to-all-start = ((bf16[16,10,2048]{2,1,0:T(8,128)(2,1)}), bf16[16,10,2048]{2,1,0:T(8,128)(2,1)S(1)}, u32[]{:S(2)}, u32[]{:S(2)}) async-start(bf16[16,10,2048]{2,1,0:T(8,128)(2,1)} %reshape.112), calls=%async_computation | async-start | bytes 2097152 | tf_op jit(solution)/shard_map/while/body/eval_jaxpr/all_to_all | solution.py:75
  428.9 21.0 %all-to-all-start.1 = ((bf16[2,80,2048]{2,0,1:T(2,128)(2,1)}), bf16[2,80,2048]{2,0,1:T(2,128)(2,1)S(1)}, u32[]{:S(2)}, u32[]{:S(2)}) async-start(bf16[2,80,2048]{2,0,1:T(2,128)(2,1)} %copy.142), calls=%async_computation.1 | async-start | bytes 1310720 | tf_op jit(solution)/shard_map/while/body/eval_jaxpr/all_to_all | solution.py:79
  451.5 5.3 collective-permute-start
  460.9 29.3 %all-to-all-start = ((bf16[16,10,2048]{2,1,0:T(8,128)(2,1)}), bf16[16,10,2048]{2,1,0:T(8,128)(2,1)S(1)}, u32[]{:S(2)}, u32[]{:S(2)}) async-start(bf16[16,10,2048]{2,1,0:T(8,128)(2,1)} %reshape.112), calls=%async_computation | async-start | bytes 2097152 | tf_op jit(solution)/shard_map/while/body/eval_jaxpr/all_to_all | solution.py:75
  501.1 21.0 %all-to-all-start.1 = ((bf16[2,80,2048]{2,0,1:T(2,128)(2,1)}), bf16[2,80,2048]{2,0,1:T(2,128)(2,1)S(1)}, u32[]{:S(2)}, u32[]{:S(2)}) async-start(bf16[2,80,2048]{2,0,1:T(2,128)(2,1)} %copy.142), calls=%async_computation.1 | async-start | bytes 1310720 | tf_op jit(solution)/shard_map/while/body/eval_jaxpr/all_to_all | solution.py:79
  523.7 5.3 collective-permute-start
  533.0 29.3 %all-to-all-start = ((bf16[16,10,2048]{2,1,0:T(8,128)(2,1)}), bf16[16,10,2048]{2,1,0:T(8,128)(2,1)S(1)}, u32[]{:S(2)}, u32[]{:S(2)}) async-start(bf16[16,10,2048]{2,1,0:T(8,128)(2,1)} %reshape.112), calls=%async_computation | async-start | bytes 2097152 | tf_op jit(solution)/shard_map/while/body/eval_jaxpr/all_to_all | solution.py:75
  573.2 21.0 %all-to-all-start.1 = ((bf16[2,80,2048]{2,0,1:T(2,128)(2,1)}), bf16[2,80,2048]{2,0,1:T(2,128)(2,1)S(1)}, u32[]{:S(2)}, u32[]{:S(2)}) async-start(bf16[2,80,2048]{2,0,1:T(2,128)(2,1)} %copy.142), calls=%async_computation.1 | async-start | bytes 1310720 | tf_op jit(solution)/shard_map/while/body/eval_jaxpr/all_to_all | solution.py:79
  595.8 5.3 collective-permute-start
  605.2 29.3 %all-to-all-start = ((bf16[16,10,2048]{2,1,0:T(8,128)(2,1)}), bf16[16,10,2048]{2,1,0:T(8,128)(2,1)S(1)}, u32[]{:S(2)}, u32[]{:S(2)}) async-start(bf16[16,10,2048]{2,1,0:T(8,128)(2,1)} %reshape.112), calls=%async_computation | async-start | bytes 2097152 | tf_op jit(solution)/shard_map/while/body/eval_jaxpr/all_to_all | solution.py:75
  638.3 21.0 %all-to-all-start.1 = ((bf16[2,80,2048]{2,0,1:T(2,128)(2,1)}), bf16[2,80,2048]{2,0,1:T(2,128)(2,1)S(1)}, u32[]{:S(2)}, u32[]{:S(2)}) async-start(bf16[2,80,2048]{2,0,1:T(2,128)(2,1)} %copy.142), calls=%async_computation.1 | async-start | bytes 1310720 | tf_op jit(solution)/shard_map/while/body/eval_jaxpr/all_to_all | solution.py:79
  660.9 12.2 collective-permute-start
  680.9 29.0 %all-to-all-start.2 = ((bf16[16,10,2048]{2,1,0:T(8,128)(2,1)}), bf16[16,10,2048]{2,1,0:T(8,128)(2,1)S(1)}, u32[]{:S(2)}, u32[]{:S(2)}) async-start(bf16[16,10,2048]{2,1,0:T(8,128)(2,1)} %reshape.114), calls=%async_computation.2 | async-start | bytes 2097152 | tf_op jit(solution)/shard_map/while/body/eval_jaxpr/all_to_all | solution.py:75
  713.5 20.8 %all-to-all-start.3 = ((bf16[2,80,2048]{2,0,1:T(2,128)(2,1)}), bf16[2,80,2048]{2,0,1:T(2,128)(2,1)S(1)}, u32[]{:S(2)}, u32[]{:S(2)}) async-start(bf16[2,80,2048]{2,0,1:T(2,128)(2,1)} %copy.148), calls=%async_computation.3 | async-start | bytes 1310720 | tf_op jit(solution)/shard_map/while/body/eval_jaxpr/all_to_all | solution.py:79
  737.0 14.2 %collective-permute-start.1 = (bf16[16,2048]{1,0:T(8,128)(2,1)S(1)}, bf16[16,2048]{1,0:T(8,128)(2,1)S(1)}, u32[]{:S(2)}, u32[]{:S(2)}) collective-permute-start(bf16[16,2048]{1,0:T(8,128)(2,1)S(1)} %get-tuple-element.1148), channel_id=1, source_target_pairs={{16,0},{17,1},{18,2},{19,3},{20,4},{21,5},{22,6},{23,7},{24,8},{25... | collective-permute-start | bytes 196616 | tf_op jit(solution)/shard_map/while/body/eval_jaxpr/ppermute | solution.py:12
  753.6 29.2 %all-to-all-start.2 = ((bf16[16,10,2048]{2,1,0:T(8,128)(2,1)}), bf16[16,10,2048]{2,1,0:T(8,128)(2,1)S(1)}, u32[]{:S(2)}, u32[]{:S(2)}) async-start(bf16[16,10,2048]{2,1,0:T(8,128)(2,1)} %reshape.114), calls=%async_computation.2 | async-start | bytes 2097152 | tf_op jit(solution)/shard_map/while/body/eval_jaxpr/all_to_all | solution.py:75
  784.1 4.8 copy-start.1
  795.1 20.9 %all-to-all-start.3 = ((bf16[2,80,2048]{2,0,1:T(2,128)(2,1)}), bf16[2,80,2048]{2,0,1:T(2,128)(2,1)S(1)}, u32[]{:S(2)}, u32[]{:S(2)}) async-start(bf16[2,80,2048]{2,0,1:T(2,128)(2,1)} %copy.148), calls=%async_computation.3 | async-start | bytes 1310720 | tf_op jit(solution)/shard_map/while/body/eval_jaxpr/all_to_all | solution.py:79
  818.7 6.2 collective-permute-start.1
  827.3 28.7 %all-to-all-start.2 = ((bf16[16,10,2048]{2,1,0:T(8,128)(2,1)}), bf16[16,10,2048]{2,1,0:T(8,128)(2,1)S(1)}, u32[]{:S(2)}, u32[]{:S(2)}) async-start(bf16[16,10,2048]{2,1,0:T(8,128)(2,1)} %reshape.114), calls=%async_computation.2 | async-start | bytes 2097152 | tf_op jit(solution)/shard_map/while/body/eval_jaxpr/all_to_all | solution.py:75
  857.1 4.8 copy-start.1
  868.2 20.9 %all-to-all-start.3 = ((bf16[2,80,2048]{2,0,1:T(2,128)(2,1)}), bf16[2,80,2048]{2,0,1:T(2,128)(2,1)S(1)}, u32[]{:S(2)}, u32[]{:S(2)}) async-start(bf16[2,80,2048]{2,0,1:T(2,128)(2,1)} %copy.148), calls=%async_computation.3 | async-start | bytes 1310720 | tf_op jit(solution)/shard_map/while/body/eval_jaxpr/all_to_all | solution.py:79
  891.8 6.2 collective-permute-start.1
  900.3 28.7 %all-to-all-start.2 = ((bf16[16,10,2048]{2,1,0:T(8,128)(2,1)}), bf16[16,10,2048]{2,1,0:T(8,128)(2,1)S(1)}, u32[]{:S(2)}, u32[]{:S(2)}) async-start(bf16[16,10,2048]{2,1,0:T(8,128)(2,1)} %reshape.114), calls=%async_computation.2 | async-start | bytes 2097152 | tf_op jit(solution)/shard_map/while/body/eval_jaxpr/all_to_all | solution.py:75
  930.2 4.8 copy-start.1
  941.3 20.9 %all-to-all-start.3 = ((bf16[2,80,2048]{2,0,1:T(2,128)(2,1)}), bf16[2,80,2048]{2,0,1:T(2,128)(2,1)S(1)}, u32[]{:S(2)}, u32[]{:S(2)}) async-start(bf16[2,80,2048]{2,0,1:T(2,128)(2,1)} %copy.148), calls=%async_computation.3 | async-start | bytes 1310720 | tf_op jit(solution)/shard_map/while/body/eval_jaxpr/all_to_all | solution.py:79
  964.8 6.2 collective-permute-start.1
  973.3 28.7 %all-to-all-start.2 = ((bf16[16,10,2048]{2,1,0:T(8,128)(2,1)}), bf16[16,10,2048]{2,1,0:T(8,128)(2,1)S(1)}, u32[]{:S(2)}, u32[]{:S(2)}) async-start(bf16[16,10,2048]{2,1,0:T(8,128)(2,1)} %reshape.114), calls=%async_computation.2 | async-start | bytes 2097152 | tf_op jit(solution)/shard_map/while/body/eval_jaxpr/all_to_all | solution.py:75
  1003.2 4.8 copy-start.1
  1014.3 20.9 %all-to-all-start.3 = ((bf16[2,80,2048]{2,0,1:T(2,128)(2,1)}), bf16[2,80,2048]{2,0,1:T(2,128)(2,1)S(1)}, u32[]{:S(2)}, u32[]{:S(2)}) async-start(bf16[2,80,2048]{2,0,1:T(2,128)(2,1)} %copy.148), calls=%async_computation.3 | async-start | bytes 1310720 | tf_op jit(solution)/shard_map/while/body/eval_jaxpr/all_to_all | solution.py:79
  1037.8 6.2 collective-permute-start.1
  1046.4 28.7 %all-to-all-start.2 = ((bf16[16,10,2048]{2,1,0:T(8,128)(2,1)}), bf16[16,10,2048]{2,1,0:T(8,128)(2,1)S(1)}, u32[]{:S(2)}, u32[]{:S(2)}) async-start(bf16[16,10,2048]{2,1,0:T(8,128)(2,1)} %reshape.114), calls=%async_computation.2 | async-start | bytes 2097152 | tf_op jit(solution)/shard_map/while/body/eval_jaxpr/all_to_all | solution.py:75
  1076.2 4.8 copy-start.1
  1087.3 20.9 %all-to-all-start.3 = ((bf16[2,80,2048]{2,0,1:T(2,128)(2,1)}), bf16[2,80,2048]{2,0,1:T(2,128)(2,1)S(1)}, u32[]{:S(2)}, u32[]{:S(2)}) async-start(bf16[2,80,2048]{2,0,1:T(2,128)(2,1)} %copy.148), calls=%async_computation.3 | async-start | bytes 1310720 | tf_op jit(solution)/shard_map/while/body/eval_jaxpr/all_to_all | solution.py:79
  1110.9 6.2 collective-permute-start.1
  1119.4 28.7 %all-to-all-start.2 = ((bf16[16,10,2048]{2,1,0:T(8,128)(2,1)}), bf16[16,10,2048]{2,1,0:T(8,128)(2,1)S(1)}, u32[]{:S(2)}, u32[]{:S(2)}) async-start(bf16[16,10,2048]{2,1,0:T(8,128)(2,1)} %reshape.114), calls=%async_computation.2 | async-start | bytes 2097152 | tf_op jit(solution)/shard_map/while/body/eval_jaxpr/all_to_all | solution.py:75
  1149.3 4.8 copy-start.1
  1160.4 20.9 %all-to-all-start.3 = ((bf16[2,80,2048]{2,0,1:T(2,128)(2,1)}), bf16[2,80,2048]{2,0,1:T(2,128)(2,1)S(1)}, u32[]{:S(2)}, u32[]{:S(2)}) async-start(bf16[2,80,2048]{2,0,1:T(2,128)(2,1)} %copy.148), calls=%async_computation.3 | async-start | bytes 1310720 | tf_op jit(solution)/shard_map/while/body/eval_jaxpr/all_to_all | solution.py:79
  1183.9 6.2 collective-permute-start.1
  1192.4 28.7 %all-to-all-start.2 = ((bf16[16,10,2048]{2,1,0:T(8,128)(2,1)}), bf16[16,10,2048]{2,1,0:T(8,128)(2,1)S(1)}, u32[]{:S(2)}, u32[]{:S(2)}) async-start(bf16[16,10,2048]{2,1,0:T(8,128)(2,1)} %reshape.114), calls=%async_computation.2 | async-start | bytes 2097152 | tf_op jit(solution)/shard_map/while/body/eval_jaxpr/all_to_all | solution.py:75
  1233.4 20.9 %all-to-all-start.3 = ((bf16[2,80,2048]{2,0,1:T(2,128)(2,1)}), bf16[2,80,2048]{2,0,1:T(2,128)(2,1)S(1)}, u32[]{:S(2)}, u32[]{:S(2)}) async-start(bf16[2,80,2048]{2,0,1:T(2,128)(2,1)} %copy.148), calls=%async_computation.3 | async-start | bytes 1310720 | tf_op jit(solution)/shard_map/while/body/eval_jaxpr/all_to_all | solution.py:79
  1256.9 6.2 collective-permute-start.1
  1265.5 28.7 %all-to-all-start.2 = ((bf16[16,10,2048]{2,1,0:T(8,128)(2,1)}), bf16[16,10,2048]{2,1,0:T(8,128)(2,1)S(1)}, u32[]{:S(2)}, u32[]{:S(2)}) async-start(bf16[16,10,2048]{2,1,0:T(8,128)(2,1)} %reshape.114), calls=%async_computation.2 | async-start | bytes 2097152 | tf_op jit(solution)/shard_map/while/body/eval_jaxpr/all_to_all | solution.py:75
  1306.4 20.9 %all-to-all-start.3 = ((bf16[2,80,2048]{2,0,1:T(2,128)(2,1)}), bf16[2,80,2048]{2,0,1:T(2,128)(2,1)S(1)}, u32[]{:S(2)}, u32[]{:S(2)}) async-start(bf16[2,80,2048]{2,0,1:T(2,128)(2,1)} %copy.148), calls=%async_computation.3 | async-start | bytes 1310720 | tf_op jit(solution)/shard_map/while/body/eval_jaxpr/all_to_all | solution.py:79
  1330.0 6.2 collective-permute-start.1
  1336.1 8.5 copy-start.6
  1344.7 26.6 %reduce-scatter.4.cloned.1.call-start = ((), (), s32[]{:S(2)}) async-start(), calls=%async_computation.7 | async-start | bytes 6291456 | tf_op jit(solution)/shard_map/reduce_scatter | solution.py:228
  1354.4 33.0 %reduce-scatter.8.cloned.1.call-start = ((), (), s32[]{:S(2)}) async-start(), calls=%async_computation.9 | async-start | bytes 6291456 | tf_op jit(solution)/shard_map/reduce_scatter | solution.py:234
  (29 other events, 85.2 us)
Sparse Core Ops, SparseCore 0:
  1344.8 10.1 reduce-scatter.5
  1357.9 13.3 reduce-scatter.3
  1374.1 13.3 reduce-scatter.7
where the time goes:
time: 1400 us; the launch traced here: 1390 us
  waiting for transfers between devices  712 us (51%)
  local copies, waits for them, and re-layouts  208 us (15%)
  matrix products  195 us (14%)
  starting transfers between devices  179 us (13%)
  other arithmetic  83.9 us (6%)
    all_to_all x18, waiting for transfers between devices, send_out(): lax.all_to_all(buffer, 'expert', split_axis=0, concat_axis=1, tiled=True)  421 us
    all_to_all x18, waiting for transfers between devices, send_back(): lax.all_to_all(buffer, 'expert', split_axis=1, concat_axis=0, tiled=True)  231 us
    dynamic_slice x81, local copies, waits for them, and re-layouts, keep_slice(): previous = lax.dynamic_index_in_dim(stored, at_index, 0, keepdims=False)  70.5 us
    all_to_all x18, starting transfers between devices, send_out(): lax.all_to_all(buffer, 'expert', split_axis=0, concat_axis=1, tiled=True)  69.2 us
    all_to_all x18, starting transfers between devices, send_back(): lax.all_to_all(buffer, 'expert', split_axis=1, concat_axis=0, tiled=True)  64.1 us
    dynamic_update_slice x36, other arithmetic, keep_slice(): lax.dynamic_update_index_in_dim(stored, jnp.where(is_valid, new_value, pr...  55.1 us
    ppermute x18, starting transfers between devices, from_behind(): return lax.ppermute(block, axis, route)  46.1 us
    dot_general x8, matrix products, expert_backward(): jnp.einsum('erx,efx->erf', out_grad, down_w, preferred_element_type=jnp.f...  38.1 us
  transfers between devices with their start and end apart: 57, of which 48 were waited for; matrix products, arithmetic and copies ran while one was open for 12% of the time, Pallas kernels for 0%

commit v1 on v0

--- a/solution.py
+++ b/solution.py
@@ -76,7 +76,12 @@
 
 
 def send_back(buffer):
-    return lax.all_to_all(buffer, "expert", split_axis=1, concat_axis=0, tiled=True)
+    return jnp.concatenate(
+        lax.all_to_all(
+            jnp.stack(jnp.split(buffer, lax.axis_size("expert"), axis=1)), "expert", 0, 0
+        ),
+        axis=0,
+    )
 
 
 def on_device(tokens_in, cotangent, routes, router_weights, norm_gain, w_gate, w_up, w_down):

time: 1400 us -> 1500 us (1.071)
  local copies, waits for them, and re-layouts: 208 us -> 312 us
  matrix products: 195 us -> 179 us
    while x0 -> x126, local copies, waits for them, and re-layouts: none -> 87.2 us
    another operation x33 -> x81, local copies, waits for them, and re-layouts: 24.9 us -> 39.9 us
  transfers between devices with their start and end apart: 57 -> 57, of which waited for: 48 -> 48; matrix products, arithmetic and copies ran while one was open for 12% -> 11% of each run, Pallas kernels for 0% -> 0%
where the time goes in v1:
time: 1500 us; the launch traced here: 1480 us
  waiting for transfers between devices  712 us (47%)
  local copies, waits for them, and re-layouts  312 us (21%)
  starting transfers between devices  181 us (12%)
  matrix products  179 us (12%)
  other arithmetic  81.8 us (5%)
    all_to_all x18, waiting for transfers between devices, send_out(): lax.all_to_all(buffer, 'expert', split_axis=0, concat_axis=1, tiled=True)  413 us
    all_to_all x18, waiting for transfers between devices, send_back(): lax.all_to_all(jnp.stack(jnp.split(buffer, lax.axis_size('expert'), axis=...  231 us
    while x126, local copies, waits for them, and re-layouts  87.2 us
    dynamic_slice x81, local copies, waits for them, and re-layouts, keep_slice(): previous = lax.dynamic_index_in_dim(stored, at_index, 0, keepdims=False)  78 us
    all_to_all x18, starting transfers between devices, send_out(): lax.all_to_all(buffer, 'expert', split_axis=0, concat_axis=1, tiled=True)  69.2 us
    all_to_all x18, starting transfers between devices, send_back(): lax.all_to_all(jnp.stack(jnp.split(buffer, lax.axis_size('expert'), axis=...  64.1 us
    dynamic_update_slice x36, other arithmetic, keep_slice(): lax.dynamic_update_index_in_dim(stored, jnp.where(is_valid, new_value, pr...  51.7 us
    ppermute x18, starting transfers between devices, from_behind(): return lax.ppermute(block, axis, route)  47.8 us
  transfers between devices with their start and end apart: 57, of which 48 were waited for; matrix products, arithmetic and copies ran while one was open for 11% of the time, Pallas kernels for 0%

profile of v1, /device:TPU:0, one launch (start us, length us, event | category | flops | bytes accessed | tf_op | source)
XLA Modules:
  0.0 1484.4 jit_solution(9513337331960689952)
XLA Ops:
  22.9 705.2 %while.47 = (s32[]{:T(128)}, bf16[16,2048]{1,0:T(8,128)(2,1)S(1)}, bf16[8,16,2048]{2,1,0:T(8,128)(2,1)}, bf16[8,2,80,2048]{3,2,0,1:T(8,128)(2,1)}, f32[8,2,80,51...) while((s32[]{:T(128)}, bf16[16,2048]{1,0:T(8,128)(2,1)S(1)}, ...), condition=%wide.region_8.9_spmd, body=%wide.region_4.0_spmd.sunk | while | flops 1082097664 | bytes 79006560 | solution.py:157
  27.6 7.3 all-to-all-start
  36.9 23.8 %all-to-all-done = bf16[16,10,2048]{2,1,0:T(8,128)(2,1)S(1)} async-done(((bf16[16,10,2048]{2,1,0:T(8,128)(2,1)}), bf16[16,10,2048]{2,1,0:T(8,128)(2,1)S(1)}, u32[]{:S(2)}, u32[]{:S(2)}) %all-to-all-start) | async-done | bytes 655392 | tf_op jit(solution)/shard_map/while/body/eval_jaxpr/all_to_all | solution.py:75
  61.4 9.2 conditional.4
  84.4 12.8 all-to-all-done.1
  113.0 24.0 %all-to-all-done = bf16[16,10,2048]{2,1,0:T(8,128)(2,1)S(1)} async-done(((bf16[16,10,2048]{2,1,0:T(8,128)(2,1)}), bf16[16,10,2048]{2,1,0:T(8,128)(2,1)S(1)}, u32[]{:S(2)}, u32[]{:S(2)}) %all-to-all-start) | async-done | bytes 655392 | tf_op jit(solution)/shard_map/while/body/eval_jaxpr/all_to_all | solution.py:75
  137.7 9.2 conditional.4
  160.7 12.9 all-to-all-done.1
  191.7 23.7 %all-to-all-done = bf16[16,10,2048]{2,1,0:T(8,128)(2,1)S(1)} async-done(((bf16[16,10,2048]{2,1,0:T(8,128)(2,1)}), bf16[16,10,2048]{2,1,0:T(8,128)(2,1)S(1)}, u32[]{:S(2)}, u32[]{:S(2)}) %all-to-all-start) | async-done | bytes 655392 | tf_op jit(solution)/shard_map/while/body/eval_jaxpr/all_to_all | solution.py:75
  216.1 9.2 conditional.4
  239.1 12.9 all-to-all-done.1
  269.9 23.7 %all-to-all-done = bf16[16,10,2048]{2,1,0:T(8,128)(2,1)S(1)} async-done(((bf16[16,10,2048]{2,1,0:T(8,128)(2,1)}), bf16[16,10,2048]{2,1,0:T(8,128)(2,1)S(1)}, u32[]{:S(2)}, u32[]{:S(2)}) %all-to-all-start) | async-done | bytes 655392 | tf_op jit(solution)/shard_map/while/body/eval_jaxpr/all_to_all | solution.py:75
  294.3 9.2 conditional.4
  317.2 12.8 all-to-all-done.1
  347.9 23.7 %all-to-all-done = bf16[16,10,2048]{2,1,0:T(8,128)(2,1)S(1)} async-done(((bf16[16,10,2048]{2,1,0:T(8,128)(2,1)}), bf16[16,10,2048]{2,1,0:T(8,128)(2,1)S(1)}, u32[]{:S(2)}, u32[]{:S(2)}) %all-to-all-start) | async-done | bytes 655392 | tf_op jit(solution)/shard_map/while/body/eval_jaxpr/all_to_all | solution.py:75
  372.3 9.2 conditional.4
  395.3 12.9 all-to-all-done.1
  426.1 23.7 %all-to-all-done = bf16[16,10,2048]{2,1,0:T(8,128)(2,1)S(1)} async-done(((bf16[16,10,2048]{2,1,0:T(8,128)(2,1)}), bf16[16,10,2048]{2,1,0:T(8,128)(2,1)S(1)}, u32[]{:S(2)}, u32[]{:S(2)}) %all-to-all-start) | async-done | bytes 655392 | tf_op jit(solution)/shard_map/while/body/eval_jaxpr/all_to_all | solution.py:75
  450.5 9.2 conditional.4
  473.4 12.9 all-to-all-done.1
  504.1 23.7 %all-to-all-done = bf16[16,10,2048]{2,1,0:T(8,128)(2,1)S(1)} async-done(((bf16[16,10,2048]{2,1,0:T(8,128)(2,1)}), bf16[16,10,2048]{2,1,0:T(8,128)(2,1)S(1)}, u32[]{:S(2)}, u32[]{:S(2)}) %all-to-all-start) | async-done | bytes 655392 | tf_op jit(solution)/shard_map/while/body/eval_jaxpr/all_to_all | solution.py:75
  528.5 9.2 conditional.4
  551.5 12.9 all-to-all-done.1
  582.2 23.7 %all-to-all-done = bf16[16,10,2048]{2,1,0:T(8,128)(2,1)S(1)} async-done(((bf16[16,10,2048]{2,1,0:T(8,128)(2,1)}), bf16[16,10,2048]{2,1,0:T(8,128)(2,1)S(1)}, u32[]{:S(2)}, u32[]{:S(2)}) %all-to-all-start) | async-done | bytes 655392 | tf_op jit(solution)/shard_map/while/body/eval_jaxpr/all_to_all | solution.py:75
  606.6 9.2 conditional.4
  629.6 12.9 all-to-all-done.1
  660.4 23.7 %all-to-all-done = bf16[16,10,2048]{2,1,0:T(8,128)(2,1)S(1)} async-done(((bf16[16,10,2048]{2,1,0:T(8,128)(2,1)}), bf16[16,10,2048]{2,1,0:T(8,128)(2,1)S(1)}, u32[]{:S(2)}, u32[]{:S(2)}) %all-to-all-start) | async-done | bytes 655392 | tf_op jit(solution)/shard_map/while/body/eval_jaxpr/all_to_all | solution.py:75
  699.7 12.9 all-to-all-done.1
  714.8 11.3 collective-permute-start
  734.3 692.4 %while.48 = (s32[]{:T(128)}, bf16[16,2048]{1,0:T(8,128)(2,1)S(1)}, bf16[8,2,80,2048]{3,2,1,0:T(8,128)(2,1)}, bf16[8,2,80,512]{3,2,0,1:T(8,128)(2,1)}, bf16[8,2,8...) while((s32[]{:T(128)}, bf16[16,2048]{1,0:T(8,128)(2,1)S(1)}, ...), condition=%wide.region_15.16_spmd, body=%wide.region_10.15_spmd.sunk | while | flops 1031094272 | bytes 79396456 | solution.py:219
  743.3 22.4 %all-to-all-done.2 = bf16[16,10,2048]{2,1,0:T(8,128)(2,1)S(1)} async-done(((bf16[16,10,2048]{2,1,0:T(8,128)(2,1)}), bf16[16,10,2048]{2,1,0:T(8,128)(2,1)S(1)}, u32[]{:S(2)}, u32[]{:S(2)}) %all-to-all-start.2) | async-done | bytes 655392 | tf_op jit(solution)/shard_map/while/body/eval_jaxpr/all_to_all | solution.py:75
  780.4 12.8 all-to-all-done.3
  798.6 12.3 collective-permute-done.1
  819.9 22.6 %all-to-all-done.2 = bf16[16,10,2048]{2,1,0:T(8,128)(2,1)S(1)} async-done(((bf16[16,10,2048]{2,1,0:T(8,128)(2,1)}), bf16[16,10,2048]{2,1,0:T(8,128)(2,1)S(1)}, u32[]{:S(2)}, u32[]{:S(2)}) %all-to-all-start.2) | async-done | bytes 655392 | tf_op jit(solution)/shard_map/while/body/eval_jaxpr/all_to_all | solution.py:75
  843.2 9.3 conditional.5
  866.1 12.8 all-to-all-done.3
  897.4 22.1 %all-to-all-done.2 = bf16[16,10,2048]{2,1,0:T(8,128)(2,1)S(1)} async-done(((bf16[16,10,2048]{2,1,0:T(8,128)(2,1)}), bf16[16,10,2048]{2,1,0:T(8,128)(2,1)S(1)}, u32[]{:S(2)}, u32[]{:S(2)}) %all-to-all-start.2) | async-done | bytes 655392 | tf_op jit(solution)/shard_map/while/body/eval_jaxpr/all_to_all | solution.py:75
  920.1 9.3 conditional.5
  943.0 12.8 all-to-all-done.3
  961.3 4.0 collective-permute-done.1
  974.3 22.1 %all-to-all-done.2 = bf16[16,10,2048]{2,1,0:T(8,128)(2,1)S(1)} async-done(((bf16[16,10,2048]{2,1,0:T(8,128)(2,1)}), bf16[16,10,2048]{2,1,0:T(8,128)(2,1)S(1)}, u32[]{:S(2)}, u32[]{:S(2)}) %all-to-all-start.2) | async-done | bytes 655392 | tf_op jit(solution)/shard_map/while/body/eval_jaxpr/all_to_all | solution.py:75
  997.0 9.3 conditional.5
  1019.9 12.8 all-to-all-done.3
  1051.2 22.1 %all-to-all-done.2 = bf16[16,10,2048]{2,1,0:T(8,128)(2,1)S(1)} async-done(((bf16[16,10,2048]{2,1,0:T(8,128)(2,1)}), bf16[16,10,2048]{2,1,0:T(8,128)(2,1)S(1)}, u32[]{:S(2)}, u32[]{:S(2)}) %all-to-all-start.2) | async-done | bytes 655392 | tf_op jit(solution)/shard_map/while/body/eval_jaxpr/all_to_all | solution.py:75
  1073.9 9.3 conditional.5
  1096.8 12.8 all-to-all-done.3
  1115.1 4.0 collective-permute-done.1
  1128.1 22.1 %all-to-all-done.2 = bf16[16,10,2048]{2,1,0:T(8,128)(2,1)S(1)} async-done(((bf16[16,10,2048]{2,1,0:T(8,128)(2,1)}), bf16[16,10,2048]{2,1,0:T(8,128)(2,1)S(1)}, u32[]{:S(2)}, u32[]{:S(2)}) %all-to-all-start.2) | async-done | bytes 655392 | tf_op jit(solution)/shard_map/while/body/eval_jaxpr/all_to_all | solution.py:75
  1150.8 9.3 conditional.5
  1173.8 12.8 all-to-all-done.3
  1205.0 22.1 %all-to-all-done.2 = bf16[16,10,2048]{2,1,0:T(8,128)(2,1)S(1)} async-done(((bf16[16,10,2048]{2,1,0:T(8,128)(2,1)}), bf16[16,10,2048]{2,1,0:T(8,128)(2,1)S(1)}, u32[]{:S(2)}, u32[]{:S(2)}) %all-to-all-start.2) | async-done | bytes 655392 | tf_op jit(solution)/shard_map/while/body/eval_jaxpr/all_to_all | solution.py:75
  1227.7 9.3 conditional.5
  1250.7 12.8 all-to-all-done.3
  1281.9 22.1 %all-to-all-done.2 = bf16[16,10,2048]{2,1,0:T(8,128)(2,1)S(1)} async-done(((bf16[16,10,2048]{2,1,0:T(8,128)(2,1)}), bf16[16,10,2048]{2,1,0:T(8,128)(2,1)S(1)}, u32[]{:S(2)}, u32[]{:S(2)}) %all-to-all-start.2) | async-done | bytes 655392 | tf_op jit(solution)/shard_map/while/body/eval_jaxpr/all_to_all | solution.py:75
  1304.6 9.3 conditional.5
  1327.5 12.8 all-to-all-done.3
  1358.8 22.1 %all-to-all-done.2 = bf16[16,10,2048]{2,1,0:T(8,128)(2,1)S(1)} async-done(((bf16[16,10,2048]{2,1,0:T(8,128)(2,1)}), bf16[16,10,2048]{2,1,0:T(8,128)(2,1)S(1)}, u32[]{:S(2)}, u32[]{:S(2)}) %all-to-all-start.2) | async-done | bytes 655392 | tf_op jit(solution)/shard_map/while/body/eval_jaxpr/all_to_all | solution.py:75
  1381.5 9.3 conditional.5
  1404.4 12.8 all-to-all-done.3
  1426.7 8.3 bitcast_convert_fusion.1
  1436.3 8.4 bitcast_convert_fusion.2
  1446.6 8.8 bitcast_convert_fusion
  1455.4 6.2 reduce-scatter.4.cloned.1.call-done
  1461.6 16.2 %reduce-scatter.8.cloned.1.call-done = bf16[2,256,2048]{2,1,0:T(8,128)(2,1)} async-done(((bf16[2,512,2048]{2,1,0:T(8,128)(2,1)}), bf16[2,256,2048]{2,1,0:T(8,128)(2,1)}) %reduce-scatter.8.cloned.1.call-update) | async-done | bytes 2097168 | tf_op jit(solution)/shard_map/reduce_scatter | solution.py:239
  (967 shorter events, 736.9 us)
Async XLA Ops:
  7.2 1448.2 %reduce-scatter.6.cloned.1.call-start = ((), (), s32[]{:S(2)}) async-start(), calls=%async_computation.8 | async-start | bytes 6291456 | tf_op jit(solution)/shard_map/reduce_scatter | solution.py:236
  27.6 33.0 %all-to-all-start = ((bf16[16,10,2048]{2,1,0:T(8,128)(2,1)}), bf16[16,10,2048]{2,1,0:T(8,128)(2,1)S(1)}, u32[]{:S(2)}, u32[]{:S(2)}) async-start(bf16[16,10,2048]{2,1,0:T(8,128)(2,1)} %reshape.110), calls=%async_computation | async-start | bytes 2097152 | tf_op jit(solution)/shard_map/while/body/eval_jaxpr/all_to_all | solution.py:75
  76.2 21.1 %all-to-all-start.1 = ((bf16[8,2,10,2048]{3,1,2,0:T(2,128)(2,1)}), bf16[8,2,10,2048]{3,1,2,0:T(2,128)(2,1)S(1)}, u32[]{:S(2)}, u32[]{:S(2)}) async-start(bf16[8,2,10,2048]{3,1,2,0:T(2,128)(2,1)} %constant_dynamic-update-slice_fusion.39), calls=%async_computation.1 | async-start | bytes 1310720 | tf_op jit(solution)/shard_map/while/body/eval_jaxpr/all_to_all | solution.py:80
  99.5 3.2 collective-permute-start
  107.4 29.6 %all-to-all-start = ((bf16[16,10,2048]{2,1,0:T(8,128)(2,1)}), bf16[16,10,2048]{2,1,0:T(8,128)(2,1)S(1)}, u32[]{:S(2)}, u32[]{:S(2)}) async-start(bf16[16,10,2048]{2,1,0:T(8,128)(2,1)} %reshape.110), calls=%async_computation | async-start | bytes 2097152 | tf_op jit(solution)/shard_map/while/body/eval_jaxpr/all_to_all | solution.py:75
  152.5 21.1 %all-to-all-start.1 = ((bf16[8,2,10,2048]{3,1,2,0:T(2,128)(2,1)}), bf16[8,2,10,2048]{3,1,2,0:T(2,128)(2,1)S(1)}, u32[]{:S(2)}, u32[]{:S(2)}) async-start(bf16[8,2,10,2048]{3,1,2,0:T(2,128)(2,1)} %constant_dynamic-update-slice_fusion.39), calls=%async_computation.1 | async-start | bytes 1310720 | tf_op jit(solution)/shard_map/while/body/eval_jaxpr/all_to_all | solution.py:80
  175.8 5.6 collective-permute-start
  186.1 29.3 %all-to-all-start = ((bf16[16,10,2048]{2,1,0:T(8,128)(2,1)}), bf16[16,10,2048]{2,1,0:T(8,128)(2,1)S(1)}, u32[]{:S(2)}, u32[]{:S(2)}) async-start(bf16[16,10,2048]{2,1,0:T(8,128)(2,1)} %reshape.110), calls=%async_computation | async-start | bytes 2097152 | tf_op jit(solution)/shard_map/while/body/eval_jaxpr/all_to_all | solution.py:75
  230.9 21.0 %all-to-all-start.1 = ((bf16[8,2,10,2048]{3,1,2,0:T(2,128)(2,1)}), bf16[8,2,10,2048]{3,1,2,0:T(2,128)(2,1)S(1)}, u32[]{:S(2)}, u32[]{:S(2)}) async-start(bf16[8,2,10,2048]{3,1,2,0:T(2,128)(2,1)} %constant_dynamic-update-slice_fusion.39), calls=%async_computation.1 | async-start | bytes 1310720 | tf_op jit(solution)/shard_map/while/body/eval_jaxpr/all_to_all | solution.py:80
  254.2 5.3 collective-permute-start
  264.2 29.3 %all-to-all-start = ((bf16[16,10,2048]{2,1,0:T(8,128)(2,1)}), bf16[16,10,2048]{2,1,0:T(8,128)(2,1)S(1)}, u32[]{:S(2)}, u32[]{:S(2)}) async-start(bf16[16,10,2048]{2,1,0:T(8,128)(2,1)} %reshape.110), calls=%async_computation | async-start | bytes 2097152 | tf_op jit(solution)/shard_map/while/body/eval_jaxpr/all_to_all | solution.py:75
  309.0 21.0 %all-to-all-start.1 = ((bf16[8,2,10,2048]{3,1,2,0:T(2,128)(2,1)}), bf16[8,2,10,2048]{3,1,2,0:T(2,128)(2,1)S(1)}, u32[]{:S(2)}, u32[]{:S(2)}) async-start(bf16[8,2,10,2048]{3,1,2,0:T(2,128)(2,1)} %constant_dynamic-update-slice_fusion.39), calls=%async_computation.1 | async-start | bytes 1310720 | tf_op jit(solution)/shard_map/while/body/eval_jaxpr/all_to_all | solution.py:80
  332.3 5.3 collective-permute-start
  342.3 29.3 %all-to-all-start = ((bf16[16,10,2048]{2,1,0:T(8,128)(2,1)}), bf16[16,10,2048]{2,1,0:T(8,128)(2,1)S(1)}, u32[]{:S(2)}, u32[]{:S(2)}) async-start(bf16[16,10,2048]{2,1,0:T(8,128)(2,1)} %reshape.110), calls=%async_computation | async-start | bytes 2097152 | tf_op jit(solution)/shard_map/while/body/eval_jaxpr/all_to_all | solution.py:75
  387.1 21.0 %all-to-all-start.1 = ((bf16[8,2,10,2048]{3,1,2,0:T(2,128)(2,1)}), bf16[8,2,10,2048]{3,1,2,0:T(2,128)(2,1)S(1)}, u32[]{:S(2)}, u32[]{:S(2)}) async-start(bf16[8,2,10,2048]{3,1,2,0:T(2,128)(2,1)} %constant_dynamic-update-slice_fusion.39), calls=%async_computation.1 | async-start | bytes 1310720 | tf_op jit(solution)/shard_map/while/body/eval_jaxpr/all_to_all | solution.py:80
  410.4 5.3 collective-permute-start
  420.4 29.3 %all-to-all-start = ((bf16[16,10,2048]{2,1,0:T(8,128)(2,1)}), bf16[16,10,2048]{2,1,0:T(8,128)(2,1)S(1)}, u32[]{:S(2)}, u32[]{:S(2)}) async-start(bf16[16,10,2048]{2,1,0:T(8,128)(2,1)} %reshape.110), calls=%async_computation | async-start | bytes 2097152 | tf_op jit(solution)/shard_map/while/body/eval_jaxpr/all_to_all | solution.py:75
  465.2 21.0 %all-to-all-start.1 = ((bf16[8,2,10,2048]{3,1,2,0:T(2,128)(2,1)}), bf16[8,2,10,2048]{3,1,2,0:T(2,128)(2,1)S(1)}, u32[]{:S(2)}, u32[]{:S(2)}) async-start(bf16[8,2,10,2048]{3,1,2,0:T(2,128)(2,1)} %constant_dynamic-update-slice_fusion.39), calls=%async_computation.1 | async-start | bytes 1310720 | tf_op jit(solution)/shard_map/while/body/eval_jaxpr/all_to_all | solution.py:80
  488.5 5.3 collective-permute-start
  498.5 29.3 %all-to-all-start = ((bf16[16,10,2048]{2,1,0:T(8,128)(2,1)}), bf16[16,10,2048]{2,1,0:T(8,128)(2,1)S(1)}, u32[]{:S(2)}, u32[]{:S(2)}) async-start(bf16[16,10,2048]{2,1,0:T(8,128)(2,1)} %reshape.110), calls=%async_computation | async-start | bytes 2097152 | tf_op jit(solution)/shard_map/while/body/eval_jaxpr/all_to_all | solution.py:75
  543.3 21.0 %all-to-all-start.1 = ((bf16[8,2,10,2048]{3,1,2,0:T(2,128)(2,1)}), bf16[8,2,10,2048]{3,1,2,0:T(2,128)(2,1)S(1)}, u32[]{:S(2)}, u32[]{:S(2)}) async-start(bf16[8,2,10,2048]{3,1,2,0:T(2,128)(2,1)} %constant_dynamic-update-slice_fusion.39), calls=%async_computation.1 | async-start | bytes 1310720 | tf_op jit(solution)/shard_map/while/body/eval_jaxpr/all_to_all | solution.py:80
  566.6 5.3 collective-permute-start
  576.6 29.3 %all-to-all-start = ((bf16[16,10,2048]{2,1,0:T(8,128)(2,1)}), bf16[16,10,2048]{2,1,0:T(8,128)(2,1)S(1)}, u32[]{:S(2)}, u32[]{:S(2)}) async-start(bf16[16,10,2048]{2,1,0:T(8,128)(2,1)} %reshape.110), calls=%async_computation | async-start | bytes 2097152 | tf_op jit(solution)/shard_map/while/body/eval_jaxpr/all_to_all | solution.py:75
  621.4 21.0 %all-to-all-start.1 = ((bf16[8,2,10,2048]{3,1,2,0:T(2,128)(2,1)}), bf16[8,2,10,2048]{3,1,2,0:T(2,128)(2,1)S(1)}, u32[]{:S(2)}, u32[]{:S(2)}) async-start(bf16[8,2,10,2048]{3,1,2,0:T(2,128)(2,1)} %constant_dynamic-update-slice_fusion.39), calls=%async_computation.1 | async-start | bytes 1310720 | tf_op jit(solution)/shard_map/while/body/eval_jaxpr/all_to_all | solution.py:80
  644.7 5.3 collective-permute-start
  654.8 29.3 %all-to-all-start = ((bf16[16,10,2048]{2,1,0:T(8,128)(2,1)}), bf16[16,10,2048]{2,1,0:T(8,128)(2,1)S(1)}, u32[]{:S(2)}, u32[]{:S(2)}) async-start(bf16[16,10,2048]{2,1,0:T(8,128)(2,1)} %reshape.110), calls=%async_computation | async-start | bytes 2097152 | tf_op jit(solution)/shard_map/while/body/eval_jaxpr/all_to_all | solution.py:75
  691.5 21.0 %all-to-all-start.1 = ((bf16[8,2,10,2048]{3,1,2,0:T(2,128)(2,1)}), bf16[8,2,10,2048]{3,1,2,0:T(2,128)(2,1)S(1)}, u32[]{:S(2)}, u32[]{:S(2)}) async-start(bf16[8,2,10,2048]{3,1,2,0:T(2,128)(2,1)} %constant_dynamic-update-slice_fusion.39), calls=%async_computation.1 | async-start | bytes 1310720 | tf_op jit(solution)/shard_map/while/body/eval_jaxpr/all_to_all | solution.py:80
  714.8 13.2 collective-permute-start
  736.7 29.0 %all-to-all-start.2 = ((bf16[16,10,2048]{2,1,0:T(8,128)(2,1)}), bf16[16,10,2048]{2,1,0:T(8,128)(2,1)S(1)}, u32[]{:S(2)}, u32[]{:S(2)}) async-start(bf16[16,10,2048]{2,1,0:T(8,128)(2,1)} %reshape.112), calls=%async_computation.2 | async-start | bytes 2097152 | tf_op jit(solution)/shard_map/while/body/eval_jaxpr/all_to_all | solution.py:75
  772.4 20.8 %all-to-all-start.3 = ((bf16[8,2,10,2048]{3,1,2,0:T(2,128)(2,1)}), bf16[8,2,10,2048]{3,1,2,0:T(2,128)(2,1)S(1)}, u32[]{:S(2)}, u32[]{:S(2)}) async-start(bf16[8,2,10,2048]{3,1,2,0:T(2,128)(2,1)} %constant_dynamic-update-slice_fusion.47), calls=%async_computation.3 | async-start | bytes 1310720 | tf_op jit(solution)/shard_map/while/body/eval_jaxpr/all_to_all | solution.py:80
  796.5 14.4 collective-permute-start.1
  813.3 29.2 %all-to-all-start.2 = ((bf16[16,10,2048]{2,1,0:T(8,128)(2,1)}), bf16[16,10,2048]{2,1,0:T(8,128)(2,1)S(1)}, u32[]{:S(2)}, u32[]{:S(2)}) async-start(bf16[16,10,2048]{2,1,0:T(8,128)(2,1)} %reshape.112), calls=%async_computation.2 | async-start | bytes 2097152 | tf_op jit(solution)/shard_map/while/body/eval_jaxpr/all_to_all | solution.py:75
  843.7 4.1 copy-start.1
  858.0 20.9 %all-to-all-start.3 = ((bf16[8,2,10,2048]{3,1,2,0:T(2,128)(2,1)}), bf16[8,2,10,2048]{3,1,2,0:T(2,128)(2,1)S(1)}, u32[]{:S(2)}, u32[]{:S(2)}) async-start(bf16[8,2,10,2048]{3,1,2,0:T(2,128)(2,1)} %constant_dynamic-update-slice_fusion.47), calls=%async_computation.3 | async-start | bytes 1310720 | tf_op jit(solution)/shard_map/while/body/eval_jaxpr/all_to_all | solution.py:80
  882.3 6.1 collective-permute-start.1
  890.8 28.7 %all-to-all-start.2 = ((bf16[16,10,2048]{2,1,0:T(8,128)(2,1)}), bf16[16,10,2048]{2,1,0:T(8,128)(2,1)S(1)}, u32[]{:S(2)}, u32[]{:S(2)}) async-start(bf16[16,10,2048]{2,1,0:T(8,128)(2,1)} %reshape.112), calls=%async_computation.2 | async-start | bytes 2097152 | tf_op jit(solution)/shard_map/while/body/eval_jaxpr/all_to_all | solution.py:75
  920.7 4.1 copy-start.1
  935.0 20.9 %all-to-all-start.3 = ((bf16[8,2,10,2048]{3,1,2,0:T(2,128)(2,1)}), bf16[8,2,10,2048]{3,1,2,0:T(2,128)(2,1)S(1)}, u32[]{:S(2)}, u32[]{:S(2)}) async-start(bf16[8,2,10,2048]{3,1,2,0:T(2,128)(2,1)} %constant_dynamic-update-slice_fusion.47), calls=%async_computation.3 | async-start | bytes 1310720 | tf_op jit(solution)/shard_map/while/body/eval_jaxpr/all_to_all | solution.py:80
  959.2 6.1 collective-permute-start.1
  967.7 28.7 %all-to-all-start.2 = ((bf16[16,10,2048]{2,1,0:T(8,128)(2,1)}), bf16[16,10,2048]{2,1,0:T(8,128)(2,1)S(1)}, u32[]{:S(2)}, u32[]{:S(2)}) async-start(bf16[16,10,2048]{2,1,0:T(8,128)(2,1)} %reshape.112), calls=%async_computation.2 | async-start | bytes 2097152 | tf_op jit(solution)/shard_map/while/body/eval_jaxpr/all_to_all | solution.py:75
  997.6 4.1 copy-start.1
  1011.9 20.9 %all-to-all-start.3 = ((bf16[8,2,10,2048]{3,1,2,0:T(2,128)(2,1)}), bf16[8,2,10,2048]{3,1,2,0:T(2,128)(2,1)S(1)}, u32[]{:S(2)}, u32[]{:S(2)}) async-start(bf16[8,2,10,2048]{3,1,2,0:T(2,128)(2,1)} %constant_dynamic-update-slice_fusion.47), calls=%async_computation.3 | async-start | bytes 1310720 | tf_op jit(solution)/shard_map/while/body/eval_jaxpr/all_to_all | solution.py:80
  1036.1 6.1 collective-permute-start.1
  1044.6 28.7 %all-to-all-start.2 = ((bf16[16,10,2048]{2,1,0:T(8,128)(2,1)}), bf16[16,10,2048]{2,1,0:T(8,128)(2,1)S(1)}, u32[]{:S(2)}, u32[]{:S(2)}) async-start(bf16[16,10,2048]{2,1,0:T(8,128)(2,1)} %reshape.112), calls=%async_computation.2 | async-start | bytes 2097152 | tf_op jit(solution)/shard_map/while/body/eval_jaxpr/all_to_all | solution.py:75
  1074.5 4.1 copy-start.1
  1088.8 20.9 %all-to-all-start.3 = ((bf16[8,2,10,2048]{3,1,2,0:T(2,128)(2,1)}), bf16[8,2,10,2048]{3,1,2,0:T(2,128)(2,1)S(1)}, u32[]{:S(2)}, u32[]{:S(2)}) async-start(bf16[8,2,10,2048]{3,1,2,0:T(2,128)(2,1)} %constant_dynamic-update-slice_fusion.47), calls=%async_computation.3 | async-start | bytes 1310720 | tf_op jit(solution)/shard_map/while/body/eval_jaxpr/all_to_all | solution.py:80
  1113.0 6.1 collective-permute-start.1
  1121.5 28.7 %all-to-all-start.2 = ((bf16[16,10,2048]{2,1,0:T(8,128)(2,1)}), bf16[16,10,2048]{2,1,0:T(8,128)(2,1)S(1)}, u32[]{:S(2)}, u32[]{:S(2)}) async-start(bf16[16,10,2048]{2,1,0:T(8,128)(2,1)} %reshape.112), calls=%async_computation.2 | async-start | bytes 2097152 | tf_op jit(solution)/shard_map/while/body/eval_jaxpr/all_to_all | solution.py:75
  1151.4 4.1 copy-start.1
  1165.7 20.9 %all-to-all-start.3 = ((bf16[8,2,10,2048]{3,1,2,0:T(2,128)(2,1)}), bf16[8,2,10,2048]{3,1,2,0:T(2,128)(2,1)S(1)}, u32[]{:S(2)}, u32[]{:S(2)}) async-start(bf16[8,2,10,2048]{3,1,2,0:T(2,128)(2,1)} %constant_dynamic-update-slice_fusion.47), calls=%async_computation.3 | async-start | bytes 1310720 | tf_op jit(solution)/shard_map/while/body/eval_jaxpr/all_to_all | solution.py:80
  1189.9 6.1 collective-permute-start.1
  1198.4 28.7 %all-to-all-start.2 = ((bf16[16,10,2048]{2,1,0:T(8,128)(2,1)}), bf16[16,10,2048]{2,1,0:T(8,128)(2,1)S(1)}, u32[]{:S(2)}, u32[]{:S(2)}) async-start(bf16[16,10,2048]{2,1,0:T(8,128)(2,1)} %reshape.112), calls=%async_computation.2 | async-start | bytes 2097152 | tf_op jit(solution)/shard_map/while/body/eval_jaxpr/all_to_all | solution.py:75
  1242.6 20.9 %all-to-all-start.3 = ((bf16[8,2,10,2048]{3,1,2,0:T(2,128)(2,1)}), bf16[8,2,10,2048]{3,1,2,0:T(2,128)(2,1)S(1)}, u32[]{:S(2)}, u32[]{:S(2)}) async-start(bf16[8,2,10,2048]{3,1,2,0:T(2,128)(2,1)} %constant_dynamic-update-slice_fusion.47), calls=%async_computation.3 | async-start | bytes 1310720 | tf_op jit(solution)/shard_map/while/body/eval_jaxpr/all_to_all | solution.py:80
  1266.8 6.1 collective-permute-start.1
  1275.3 28.7 %all-to-all-start.2 = ((bf16[16,10,2048]{2,1,0:T(8,128)(2,1)}), bf16[16,10,2048]{2,1,0:T(8,128)(2,1)S(1)}, u32[]{:S(2)}, u32[]{:S(2)}) async-start(bf16[16,10,2048]{2,1,0:T(8,128)(2,1)} %reshape.112), calls=%async_computation.2 | async-start | bytes 2097152 | tf_op jit(solution)/shard_map/while/body/eval_jaxpr/all_to_all | solution.py:75
  1305.2 4.1 copy-start.1
  1319.5 20.9 %all-to-all-start.3 = ((bf16[8,2,10,2048]{3,1,2,0:T(2,128)(2,1)}), bf16[8,2,10,2048]{3,1,2,0:T(2,128)(2,1)S(1)}, u32[]{:S(2)}, u32[]{:S(2)}) async-start(bf16[8,2,10,2048]{3,1,2,0:T(2,128)(2,1)} %constant_dynamic-update-slice_fusion.47), calls=%async_computation.3 | async-start | bytes 1310720 | tf_op jit(solution)/shard_map/while/body/eval_jaxpr/all_to_all | solution.py:80
  1343.7 6.1 collective-permute-start.1
  1352.2 28.7 %all-to-all-start.2 = ((bf16[16,10,2048]{2,1,0:T(8,128)(2,1)}), bf16[16,10,2048]{2,1,0:T(8,128)(2,1)S(1)}, u32[]{:S(2)}, u32[]{:S(2)}) async-start(bf16[16,10,2048]{2,1,0:T(8,128)(2,1)} %reshape.112), calls=%async_computation.2 | async-start | bytes 2097152 | tf_op jit(solution)/shard_map/while/body/eval_jaxpr/all_to_all | solution.py:75
  1382.1 4.1 copy-start.1
  1396.4 20.9 %all-to-all-start.3 = ((bf16[8,2,10,2048]{3,1,2,0:T(2,128)(2,1)}), bf16[8,2,10,2048]{3,1,2,0:T(2,128)(2,1)S(1)}, u32[]{:S(2)}, u32[]{:S(2)}) async-start(bf16[8,2,10,2048]{3,1,2,0:T(2,128)(2,1)} %constant_dynamic-update-slice_fusion.47), calls=%async_computation.3 | async-start | bytes 1310720 | tf_op jit(solution)/shard_map/while/body/eval_jaxpr/all_to_all | solution.py:80
  1420.6 6.1 collective-permute-start.1
  1435.0 26.6 %reduce-scatter.4.cloned.1.call-start = ((), (), s32[]{:S(2)}) async-start(), calls=%async_computation.7 | async-start | bytes 6291456 | tf_op jit(solution)/shard_map/reduce_scatter | solution.py:233
  1444.8 33.0 %reduce-scatter.8.cloned.1.call-start = ((), (), s32[]{:S(2)}) async-start(), calls=%async_computation.9 | async-start | bytes 6291456 | tf_op jit(solution)/shard_map/reduce_scatter | solution.py:239
  (76 other events, 134.2 us)
Sparse Core Ops, SparseCore 0:
  1435.2 10.1 reduce-scatter.5
  1448.2 13.3 reduce-scatter.3
  1464.5 13.3 reduce-scatter.7
